TPU v7x, 32 devices: a whole 2x2x4 slice. The times are simulated.
32 devices in a mesh: ctx: 4 (over z), head: 4 (over x, core), rep: 2 (over y).
Axes of the slice: x: 2, y: 2, z: 4, core: 2. Of those that a mesh axis runs over, the one named last changes fastest.
Arguments:
- queries: bfloat16 [4, 256, 2048], P('rep', 'ctx', 'head'), may hold values from -6 to 6
- keyvals: bfloat16 [4, 256, 4, 128], P('rep', 'ctx', 'head'), may hold values from -6 to 6
- sinks: float32 [32], P('head'), may hold values from -1 to 3
- stream: bfloat16 [4, 256, 2880], P('rep', 'ctx', 'head'), may hold values from -6 to 6
- out_weight: bfloat16 [2048, 2880], P('head', 'ctx'), may hold values from -0.75 to 0.75
- norm_gain: float32 [2880], replicated, may hold values from 0.1 to 1.9
- router: bfloat16 [2880, 32], replicated, may hold values from -0.12 to 0.12
- expert_ids: int32 [4, 256, 4], P('rep', 'ctx'), may hold values from 0 to 31, all different within a row; in each aligned block of 64 rows (0 to 63, 64 to 127, ..., all dimensions but the last counted through in order) at most 12 rows name the same one
- w_gate_up: bfloat16 [64, 720, 5760], P('ctx', 'head'), may hold values from -0.109375 to 0.109375
- w_down: bfloat16 [64, 720, 2880], P('ctx', None, 'head'), may hold values from -0.15625 to 0.15625
Outputs:
- layer_out: bfloat16 [4, 256, 2880], P('rep', 'ctx', 'head')
Inputs may be any that keep to these rules, and one draw needn't show every extreme that they name: `expert_ids`: each position names 4 different experts. Within each aligned block of 64 positions of a sequence no expert is named by more than 12 positions, and in every draw some block has an expert named by exactly 12.
All inputs are finite; a program needn't handle non-finite values.
Results may differ from a plain program's by a relative error of at most 0.015.
Values may be sent and summed in bfloat16 or wider, within the bound.
A program may use at most 192 MiB of HBM per device.

v0:
```python
import jax
import jax.numpy as jnp
from jax import lax
from jax.sharding import PartitionSpec as P


def on_device(
    queries, keyvals, sinks, stream, out_weight, norm_gain, router, expert_ids, w_gate_up, w_down
):
    ctx_count = lax.axis_size("ctx")
    rep_count = lax.axis_size("rep")
    local_seqs = queries.shape[0]
    tokens = queries.shape[1]
    row_count = local_seqs * tokens
    kv_local = keyvals.shape[2]
    head_dim = keyvals.shape[3] // 2
    q_local = queries.shape[2] // head_dim
    query_group_size = q_local // kv_local
    wide_rows = query_group_size * tokens
    col_width = stream.shape[2]
    first_pos = lax.axis_index("ctx") * tokens
    last_pos = first_pos + tokens - 1
    score_scale = head_dim ** (-0.5)
    scaled_queries = queries * jnp.asarray(score_scale, jnp.bfloat16)
    query_grid = scaled_queries.reshape(local_seqs, tokens, kv_local, query_group_size, head_dim)
    query_wide = jnp.transpose(query_grid, (0, 2, 3, 1, 4)).reshape(
        local_seqs, kv_local, wide_rows, head_dim
    )
    positions = first_pos + jnp.tile(jnp.arange(tokens), query_group_size)
    sink_rows = jnp.repeat(sinks.reshape(kv_local, query_group_size), tokens, axis=1)
    sink_grid = jnp.broadcast_to(sink_rows[None], (local_seqs, kv_local, wide_rows))
    start_state = (
        sink_grid,
        jnp.ones_like(sink_grid),
        jnp.zeros((local_seqs, kv_local, head_dim, wide_rows), jnp.float32),
    )
    gate_up_weights = w_gate_up.reshape(
        w_gate_up.shape[0], w_gate_up.shape[1], 2, w_gate_up.shape[2] // 2
    )

    def attend_block(running, shard_piece):
        peak_old, denom_old, accum_old = running
        key_block = shard_piece[..., :head_dim]
        value_block = shard_piece[..., head_dim:]
        scores = jnp.einsum(
            "skmd,snkd->sknm", query_wide, key_block, preferred_element_type=jnp.float32
        )
        key_pos = jnp.arange(shard_piece.shape[1])
        visible = key_pos[:, None] <= positions[None, :]
        masked = jnp.where(visible[None, None], scores, -jnp.inf)
        peak_new = jnp.maximum(peak_old, jnp.max(masked, axis=2))
        exp_terms = jnp.exp(masked - peak_new[:, :, None, :])
        factor = jnp.exp(peak_old - peak_new)
        denom_new = denom_old * factor + jnp.sum(exp_terms, axis=2)
        accum_new = accum_old * factor[:, :, None, :] + jnp.einsum(
            "sknm,snkd->skdm",
            exp_terms.astype(jnp.bfloat16),
            value_block,
            preferred_element_type=jnp.float32,
        )
        return (peak_new, denom_new, accum_new)

    shard_piece = lax.all_gather(keyvals, "ctx", axis=1, tiled=True)

    def keep_state(state_in):
        return state_in

    def update_state(state_in):
        return attend_block(state_in, shard_piece)

    peak_fin, denom_fin, accum_fin = lax.cond(
        jnp.int32(0) > last_pos, keep_state, update_state, start_state
    )
    normalized = (accum_fin / denom_fin[:, :, None, :]).reshape(
        local_seqs, kv_local, head_dim, query_group_size, tokens
    )
    attended = (
        jnp.transpose(normalized, (0, 4, 1, 3, 2))
        .reshape(row_count, q_local * head_dim)
        .astype(jnp.bfloat16)
    )
    partial_proj = jnp.dot(
        attended,
        lax.all_gather(out_weight, "ctx", axis=1, tiled=True),
        preferred_element_type=jnp.float32,
    )
    col_start = lax.axis_index("head") * col_width
    own_stream = stream.reshape(row_count, col_width).astype(jnp.float32)
    own_cols = lax.dynamic_slice_in_dim(partial_proj, col_start, col_width, 1) + own_stream
    placed = lax.dynamic_update_slice_in_dim(partial_proj, own_cols, col_start, 1)
    hidden_state = lax.psum(placed.astype(jnp.bfloat16), "head")
    state_float = hidden_state.astype(jnp.float32)
    inverse = lax.rsqrt(jnp.mean(state_float * state_float, axis=-1, keepdims=True) + 1e-05)
    send_rows = (state_float * inverse * norm_gain).astype(jnp.bfloat16)
    logits = jnp.dot(send_rows, router, preferred_element_type=jnp.float32)
    own_state = lax.dynamic_slice_in_dim(hidden_state, col_start, col_width, 1)
    expert_rows = expert_ids.reshape(row_count, expert_ids.shape[2])
    expert_count = router.shape[1]
    top_count = expert_rows.shape[1]
    member = expert_rows[:, :, None] == jnp.arange(expert_count)[None, None, :]
    chosen = jnp.sum(jnp.where(member, logits[:, None, :], 0.0), axis=-1)
    mix_weights = jax.nn.softmax(chosen, axis=-1)
    block_rows = row_count // rep_count
    member_int = member.astype(jnp.int32).reshape(rep_count, block_rows * top_count, expert_count)
    earlier = jnp.cumsum(member_int, axis=1) - member_int
    slot_rank = jnp.sum(earlier * member_int, axis=-1).reshape(row_count, top_count)
    target_rep = (jnp.arange(row_count) // block_rows)[:, None]
    local_halves = w_gate_up.shape[0]
    capacity = 3 * tokens // 16
    slot_total = ctx_count * rep_count * local_halves * capacity
    slot_lists = []
    for half_index in range(2):
        weight_row = 2 * expert_rows + half_index
        target_rank = weight_row // local_halves * rep_count + target_rep
        slot_lists.append(
            (target_rank * local_halves + weight_row % local_halves) * capacity + slot_rank
        )
    slot_index = jnp.stack(slot_lists, axis=-1)
    row_ids = jnp.broadcast_to(jnp.arange(row_count)[:, None, None], slot_index.shape)
    spread = (
        jnp.zeros((slot_total, row_count), jnp.bfloat16)
        .at[slot_index.reshape(-1), row_ids.reshape(-1)]
        .set(1.0)
    )
    outgoing = jnp.dot(spread, send_rows, preferred_element_type=jnp.float32).astype(jnp.bfloat16)
    outgoing = outgoing.reshape(ctx_count * rep_count, local_halves, capacity, send_rows.shape[1])
    gate_up = jnp.einsum(
        "sgcd,ghzd->sgczh",
        lax.all_to_all(outgoing, ("ctx", "rep"), split_axis=0, concat_axis=0, tiled=True),
        gate_up_weights,
        preferred_element_type=jnp.float32,
    )
    gate_part = gate_up[:, :, :, 0]
    up_part = gate_up[:, :, :, 1]
    active = (gate_part * jax.nn.sigmoid(1.702 * gate_part) * (up_part + 1.0)).astype(jnp.bfloat16)
    expert_out = jnp.einsum(
        "sgch,ghd->sgcd",
        lax.all_gather(active, "head", axis=3, tiled=True),
        w_down,
        preferred_element_type=jnp.float32,
    ).astype(jnp.bfloat16)
    returned = lax.all_to_all(expert_out, ("ctx", "rep"), split_axis=0, concat_axis=0, tiled=True)
    returned_rows = returned.reshape(slot_total, col_width)
    picked_rows = returned_rows[slot_index]
    combined = jnp.sum(mix_weights[:, :, None, None] * picked_rows.astype(jnp.float32), axis=(1, 2))
    layer_out = (own_state.astype(jnp.float32) + combined).astype(jnp.bfloat16)
    return layer_out.reshape(local_seqs, tokens, col_width)


def solution(mesh):
    placed = (
        P("rep", "ctx", "head"),
        P("rep", "ctx", "head", None),
        P("head"),
        P("rep", "ctx", "head"),
        P("head", "ctx"),
        P(),
        P(),
        P("rep", "ctx", None),
        P("ctx", "head", None),
        P("ctx", None, "head"),
    )
    return jax.shard_map(
        on_device, mesh=mesh, in_specs=placed, out_specs=P("rep", "ctx", "head"), check_vma=False
    )
```

profile of v0, /device:TPU:0, one launch (start us, length us, event | category | flops | bytes accessed | tf_op | source)
XLA Modules:
  0.0 661.9 jit_solution(3322971049654471776)
XLA Ops:
  9.9 1.2 reduce-window.6
  12.8 16.1 %all_gather.9 = bf16[2,256,1,128]{3,0,2,1:T(2,128)(2,1)S(1)} all-gather(bf16[2,64,1,128]{3,0,2,1:T(2,128)(2,1)S(1)} %copy.70), channel_id=1, replica_groups=mesh['ctx'=4,'head'=4,'rep'=2] {'ctx'}, dimensions={1}, use_global_device_ids=true | all-gather | bytes 163840 | tf_op jit(solution)/shard_map/all_gather | solution.py:63
  28.9 2.4 conditional.1
  33.0 39.7 %all-gather.3.cloned.1.call-done = bf16[512,2880]{0,1:T(8,128)(2,1)} async-done(((bf16[512,720]{0,1:T(8,128)(2,1)}), bf16[512,2880]{0,1:T(8,128)(2,1)}) %all-gather.3.cloned.1.call-update) | async-done | bytes 2949136 | tf_op jit(solution)/shard_map/all_gather | solution.py:84
  72.8 2.8 fusion.54
  76.8 8.2 %scatter_custom_fusion = bf16[196608]{0:T(1024)(128)(2,1)S(1)} fusion(s32[1024]{0:T(1024)S(1)} %broadcast_select_fusion, bf16[1024]{0:T(1024)(128)(2,1)S(1)} %broadcast.896, bf16[]{:T(256)} %constant.105.clone.1), kind=kCustom, calls=%fused_computation.44 | custom fusion | bytes 393218
  85.1 24.8 %all-reduce.2.cloned.1.call-done = bf16[128,2880]{0,1:T(8,128)(2,1)} async-done(((bf16[128,2880]{0,1:T(8,128)(2,1)}), bf16[128,2880]{0,1:T(8,128)(2,1)}) %all-reduce.2.cloned.1.call-update) | async-done | bytes 737296 | tf_op jit(solution)/shard_map/psum | solution.py:91
  109.9 1.5 fusion.22
  111.4 7.0 %convolution_convert_fusion = bf16[1536,2880]{0,1:T(8,128)(2,1)} fusion(bf16[196608]{0:T(1024)(128)(2,1)S(1)} %scatter_custom_fusion, bf16[128,2880]{0,1:T(8,128)(2,1)} %all-reduce.2.cloned.1.call-done, f32[2880]{0:T(1024)S(1)} %copy-done.4, f32[128]{0:T(128)S(1)} %add_rsqrt_fusion), kind=kOutput, calls=%fused_computation.24 | convolution fusion | flops 1138360320 | bytes 9989888 | tf_op jit(solution)/shard_map/dot_general | solution.py:125
  118.5 12.5 %copy.84 = bf16[1536,2880]{1,0:T(8,128)(2,1)} copy(bf16[1536,2880]{0,1:T(8,128)(2,1)} %convolution_convert_fusion) | data formatting | bytes 17694720 | tf_op jit(solution)/shard_map/convert_element_type | solution.py:125
  131.0 13.4 %reshape.727 = bf16[8,16,12,2880]{3,2,1,0:T(8,128)(2,1)} reshape(bf16[1536,2880]{1,0:T(8,128)(2,1)} %copy.84) | data formatting | bytes 17694720 | tf_op jit(solution)/shard_map/reshape | solution.py:126
  144.4 9.7 %copy.85 = bf16[8,16,12,2880]{3,1,2,0:T(8,128)(2,1)} copy(bf16[8,16,12,2880]{3,2,1,0:T(8,128)(2,1)} %reshape.727) | data formatting | bytes 17694720 | tf_op jit(solution)/shard_map/reshape | solution.py:126
  154.1 5.5 all-to-all-start
  159.7 55.8 %reshape.728 = bf16[16,180,2,2880]{3,2,0,1:T(2,128)(2,1)} reshape(bf16[16,180,5760]{2,0,1:T(8,128)(2,1)} %param.20) | data formatting | bytes 66355200 | tf_op jit(solution)/shard_map/reshape | solution.py:37
  215.5 140.7 %all-to-all-done = bf16[8,16,12,2880]{3,1,2,0:T(8,128)(2,1)} async-done(((bf16[8,16,12,2880]{3,1,2,0:T(8,128)(2,1)}), bf16[8,16,12,2880]{3,1,2,0:T(8,128)(2,1)}, u32[]{:S(2)}, u32[]{:S(2)}) %all-to-all-start) | async-done | bytes 8847392 | tf_op jit(solution)/shard_map/all_to_all | solution.py:129
  356.1 43.2 %fusion.14 = f32[8,16,12,2,180]{4,2,3,0,1:T(8,128)S(1)} fusion(bf16[16,180,2,2880,1]{3,2,0,1,4:T(2,128)(2,1)} %bitcast.104, bf16[8,16,12,2880,1]{3,1,2,0,4:T(8,128)(2,1)} %bitcast.12), kind=kOutput, calls=%fused_computation.27 | convolution fusion | flops 3185049600 | bytes 44236800 | tf_op jit(solution)/shard_map/sgcd,ghzd->sgczh/dot_general | solution.py:127
  399.3 1.6 fusion.21
  401.0 15.0 %copy.89 = bf16[8,16,12,180]{1,0,2,3:T(8,128)(2,1)} copy(bf16[8,16,12,180]{3,2,0,1:T(8,128)(2,1)} %fusion.21) | data formatting | bytes 1105920 | tf_op jit(solution)/shard_map/convert_element_type | solution.py:135
  416.0 112.2 %all-gather.5.cloned.1.call-done = bf16[8,16,12,720]{1,0,2,3:T(8,128)(2,1)} async-done(((bf16[8,16,12,180]{1,0,2,3:T(8,128)(2,1)}), bf16[8,16,12,720]{1,0,2,3:T(8,128)(2,1)}) %all-gather.5.cloned.1.call-update) | async-done | bytes 2211856 | tf_op jit(solution)/shard_map/all_gather | solution.py:138
  528.2 34.0 %copy.90 = bf16[8,16,12,720]{3,2,0,1:T(8,128)(2,1)S(1)} copy(bf16[8,16,12,720]{1,0,2,3:T(8,128)(2,1)} %all-gather.5.cloned.1.call-done) | data formatting | bytes 4423680 | tf_op jit(solution)/shard_map/all_gather | solution.py:138
  562.3 8.8 %convert_bitcast_fusion = bf16[8,16,12,720]{3,2,0,1:T(8,128)(2,1)S(1)} fusion(bf16[8,16,12,720]{3,2,0,1:T(8,128)(2,1)S(1)} %copy.90, bf16[16,720,720]{2,1,0:T(8,128)(2,1)} %param.21), kind=kOutput, calls=%fused_computation.26 | convolution fusion | flops 1593630720 | bytes 21012480 | tf_op jit(solution)/shard_map/sgch,ghd->sgcd/dot_general | solution.py:136
  571.0 2.7 copy.91
  573.8 5.9 all-to-all-start.1
  580.8 1.3 fusion.27
  583.0 50.9 %all-to-all-done.1 = bf16[8,16,12,720]{3,1,2,0:T(8,128)(2,1)S(1)} async-done(((bf16[8,16,12,720]{3,1,2,0:T(8,128)(2,1)}), bf16[8,16,12,720]{3,1,2,0:T(8,128)(2,1)S(1)}, u32[]{:S(2)}, u32[]{:S(2)}) %all-to-all-start.1) | async-done | bytes 2211872 | tf_op jit(solution)/shard_map/all_to_all | solution.py:142
  633.9 2.6 copy.92
  636.4 4.0 reshape.729
  640.4 5.2 gather_fusion
  645.7 3.5 reshape.751
  649.2 3.0 multiply_reduce_fusion
  652.1 1.2 copy.94
  653.3 1.0 add_convert_fusion
  (85 shorter events, 13.1 us)
Async XLA Ops:
  6.5 574.2 %copy-start = (bf16[2880,32]{0,1:T(8,128)(2,1)S(1)}, bf16[2880,32]{0,1:T(8,128)(2,1)}, u32[]{:S(2)}) copy-start(bf16[2880,32]{0,1:T(8,128)(2,1)} %param.18) | copy-start | bytes 552964
  6.5 66.2 %all-gather.3.cloned.1.call-start = ((), (), s32[]{:S(2)}) async-start(), calls=%async_computation.2 | async-start | bytes 3686400 | tf_op jit(solution)/shard_map/all_gather | solution.py:84
  7.3 102.7 %all-reduce.2.cloned.1.call-start = ((), (), s32[]{:S(2)}) async-start(), calls=%async_computation.3 | async-start | bytes 1474560 | tf_op jit(solution)/shard_map/psum | solution.py:91
  28.9 3.9 copy-start.2
  75.5 1.1 copy-start.7
  75.5 1.2 copy-start.6
  75.6 35.9 %copy-start.4 = (f32[2880]{0:T(1024)S(1)}, f32[2880]{0:T(1024)}, u32[]{:S(2)}) copy-start(f32[2880]{0:T(1024)} %param.17) | copy-start | bytes 34564
  111.4 7.1 %copy-start.5 = (f32[128]{0:T(128)}, f32[128]{0:T(128)S(1)}, u32[]{:S(2)}) copy-start(f32[128]{0:T(128)S(1)} %add_rsqrt_fusion) | copy-start | bytes 1540
  154.1 202.0 %all-to-all-start = ((bf16[8,16,12,2880]{3,1,2,0:T(8,128)(2,1)}), bf16[8,16,12,2880]{3,1,2,0:T(8,128)(2,1)}, u32[]{:S(2)}, u32[]{:S(2)}) async-start(bf16[8,16,12,2880]{3,1,2,0:T(8,128)(2,1)} %copy.85), calls=%async_computation | async-start | bytes 18087936 | tf_op jit(solution)/shard_map/all_to_all | solution.py:129
  159.7 368.6 %all-gather.5.cloned.1.call-start = ((), (), s32[]{:S(2)}) async-start(), calls=%async_computation.4 | async-start | bytes 22118400 | tf_op jit(solution)/shard_map/all_gather | solution.py:138
  573.8 5.9 copy-start.3
  573.8 7.0 %copy-start.1 = (bf16[128,2880]{0,1:T(8,128)(2,1)S(1)}, bf16[128,2880]{0,1:T(8,128)(2,1)}, u32[]{:S(2)}) copy-start(bf16[128,2880]{0,1:T(8,128)(2,1)} %all-reduce.2.cloned.1.call-done) | copy-start | bytes 2211844
  573.8 60.1 %all-to-all-start.1 = ((bf16[8,16,12,720]{3,1,2,0:T(8,128)(2,1)}), bf16[8,16,12,720]{3,1,2,0:T(8,128)(2,1)S(1)}, u32[]{:S(2)}, u32[]{:S(2)}) async-start(bf16[8,16,12,720]{3,1,2,0:T(8,128)(2,1)} %copy.91), calls=%async_computation.1 | async-start | bytes 4718592 | tf_op jit(solution)/shard_map/all_to_all | solution.py:142
Sparse Core Ops, SparseCore 0:
  8.9 63.8 all-gather.2
  76.7 33.1 all-reduce.1
  416.1 112.0 all-gather.4
where the time goes:
time: 671 us; the launch traced here: 662 us
  waiting for transfers between devices  369 us (55%)
  local copies, waits for them, and re-layouts  175 us (26%)
  matrix products  63.7 us (9%)
  blocking collectives  16.1 us (2%)
  between operations  13.7 us (2%)
  other arithmetic  12.4 us (2%)
  starting transfers between devices  11.5 us (2%)
    all_to_all x1, waiting for transfers between devices, on_device(): lax.all_to_all(outgoing, ('ctx', 'rep'), split_axis=0, concat_axis=0, til...  141 us
    all_gather x1, waiting for transfers between devices, on_device(): lax.all_gather(active, 'head', axis=3, tiled=True)  112 us
    reshape x1, local copies, waits for them, and re-layouts, on_device(): w_gate_up.reshape(w_gate_up.shape[0], w_gate_up.shape[1], 2, w_gate_up.sh...  55.8 us
    all_to_all x1, waiting for transfers between devices, on_device(): lax.all_to_all(expert_out, ('ctx', 'rep'), split_axis=0, concat_axis=0, t...  50.9 us
    dot_general x1, matrix products, on_device(): jnp.einsum('sgcd,ghzd->sgczh', lax.all_to_all(outgoing, ('ctx', 'rep'), s...  43.2 us
    all_gather x1, waiting for transfers between devices, on_device(): lax.all_gather(out_weight, 'ctx', axis=1, tiled=True)  39.7 us
    all_gather x1, local copies, waits for them, and re-layouts, on_device(): lax.all_gather(active, 'head', axis=3, tiled=True)  34 us
    psum x1, waiting for transfers between devices, on_device(): hidden_state = lax.psum(placed.astype(jnp.bfloat16), 'head')  24.8 us
  transfers between devices with their start and end apart: 5, of which 5 were waited for; matrix products, arithmetic and copies ran while one was open for 12% of the time, Pallas kernels for 0%

commit v1 on v0

--- a/solution.py
+++ b/solution.py
@@ -2,6 +2,23 @@
 import jax.numpy as jnp
 from jax import lax
 from jax.sharding import PartitionSpec as P
+
+
+def fit_unit(s0, across, axis_k):
+    right_arr, z_new, s_next = (lax.psum(1, across), lax.axis_index(across), s0.shape[axis_k])
+    kept_arr, b_now = (s0, 1)
+    while b_now < right_arr:
+        kept_arr = jnp.concatenate(
+            [
+                kept_arr,
+                lax.ppermute(
+                    kept_arr, across, [(q, (q - b_now) % right_arr) for q in range(right_arr)]
+                ),
+            ],
+            axis=axis_k,
+        )
+        b_now = 2 * b_now
+    return jnp.roll(kept_arr, z_new * s_next, axis=axis_k)
 
 
 def on_device(
@@ -135,7 +152,7 @@
     active = (gate_part * jax.nn.sigmoid(1.702 * gate_part) * (up_part + 1.0)).astype(jnp.bfloat16)
     expert_out = jnp.einsum(
         "sgch,ghd->sgcd",
-        lax.all_gather(active, "head", axis=3, tiled=True),
+        fit_unit(active, "head", axis_k=3),
         w_down,
         preferred_element_type=jnp.float32,
     ).astype(jnp.bfloat16)

time: 671 us -> 568 us (0.85)
  waiting for transfers between devices: 369 us -> 285 us
  local copies, waits for them, and re-layouts: 175 us -> 153 us
    all_gather x1 -> x0, waiting for transfers between devices: 112 us -> none  [on_device(): lax.all_gather(active, 'head', axis=3, tiled=True)]
    ppermute x0 -> x2, waiting for transfers between devices: none -> 37.1 us  [fit_unit(): lax.ppermute(kept_arr, across, [(q, (q - b_now) % right_arr) for q in ran...]
    all_gather x1 -> x0, local copies, waits for them, and re-layouts: 34 us -> none  [on_device(): lax.all_gather(active, 'head', axis=3, tiled=True)]
    convert_element_type x1, local copies, waits for them, and re-layouts: 15 us -> 0.44 us  [on_device(): (gate_part * jax.nn.sigmoid(1.702 * gate_part) * (up_part + 1.0)).astype(...]
    concatenate x0 -> x2, local copies, waits for them, and re-layouts: none -> 12.2 us  [the longest x1 11.5 us: fit_unit(): return jnp.roll(kept_arr, z_new * s_next, axis=axis_k)]
    unnamed x21 -> x27, local copies, waits for them, and re-layouts: 9.86 us -> 21 us
    psum x1, waiting for transfers between devices: 24.8 us -> 13.6 us  [on_device(): hidden_state = lax.psum(placed.astype(jnp.bfloat16), 'head')]
  transfers between devices with their start and end apart: 5 -> 6, of which waited for: 5 -> 6; matrix products, arithmetic and copies ran while one was open for 12% -> 15% of each run, Pallas kernels for 0% -> 0%
where the time goes in v1:
time: 568 us; the launch traced here: 559 us
  waiting for transfers between devices  285 us (50%)
  local copies, waits for them, and re-layouts  153 us (27%)
  matrix products  66.7 us (12%)
  blocking collectives  15.9 us (3%)
  between operations  14.2 us (2%)
  other arithmetic  12.6 us (2%)
  starting transfers between devices  11.4 us (2%)
    all_to_all x1, waiting for transfers between devices, on_device(): lax.all_to_all(outgoing, ('ctx', 'rep'), split_axis=0, concat_axis=0, til...  141 us
    reshape x1, local copies, waits for them, and re-layouts, on_device(): w_gate_up.reshape(w_gate_up.shape[0], w_gate_up.shape[1], 2, w_gate_up.sh...  55.8 us
    all_to_all x1, waiting for transfers between devices, on_device(): lax.all_to_all(expert_out, ('ctx', 'rep'), split_axis=0, concat_axis=0, t...  50.8 us
    dot_general x1, matrix products, on_device(): jnp.einsum('sgcd,ghzd->sgczh', lax.all_to_all(outgoing, ('ctx', 'rep'), s...  45.2 us
    all_gather x1, waiting for transfers between devices, on_device(): lax.all_gather(out_weight, 'ctx', axis=1, tiled=True)  42.1 us
    ppermute x2, waiting for transfers between devices, fit_unit(): lax.ppermute(kept_arr, across, [(q, (q - b_now) % right_arr) for q in ran...  37.1 us
    reshape x2, local copies, waits for them, and re-layouts, on_device(): outgoing.reshape(ctx_count * rep_count, local_halves, capacity, send_rows...  23.2 us
    unnamed x27, local copies, waits for them, and re-layouts  21 us
  transfers between devices with their start and end apart: 6, of which 6 were waited for; matrix products, arithmetic and copies ran while one was open for 15% of the time, Pallas kernels for 0%

profile of v1, /device:TPU:0, one launch (start us, length us, event | category | flops | bytes accessed | tf_op | source)
XLA Modules:
  0.0 558.7 jit_solution(396669628054109797)
XLA Ops:
  8.4 1.2 reduce-window.6
  12.0 15.9 %all_gather.6 = bf16[2,256,1,128]{3,0,2,1:T(2,128)(2,1)S(1)} all-gather(bf16[2,64,1,128]{3,0,2,1:T(2,128)(2,1)S(1)} %copy.75), channel_id=1, replica_groups=mesh['ctx'=4,'head'=4,'rep'=2] {'ctx'}, dimensions={1}, use_global_device_ids=true | all-gather | bytes 163840 | tf_op jit(solution)/shard_map/all_gather | solution.py:80
  27.9 1.8 conditional.1
  30.6 42.1 %all-gather.2.cloned.1.call-done = bf16[512,2880]{0,1:T(8,128)(2,1)} async-done(((bf16[512,720]{0,1:T(8,128)(2,1)}), bf16[512,2880]{0,1:T(8,128)(2,1)}) %all-gather.2.cloned.1.call-update) | async-done | bytes 2949136 | tf_op jit(solution)/shard_map/all_gather | solution.py:101
  72.7 2.8 fusion.58
  76.8 19.6 %scatter_custom_fusion = bf16[196608]{0:T(1024)(128)(2,1)S(1)} fusion(s32[1024]{0:T(1024)S(1)} %broadcast_select_fusion, bf16[1024]{0:T(1024)(128)(2,1)S(1)} %broadcast.896, bf16[]{:T(256)} %constant.122.clone.1), kind=kCustom, calls=%fused_computation.46 | custom fusion | bytes 393218
  96.3 13.6 %all-reduce.2.cloned.1.call-done = bf16[128,2880]{0,1:T(8,128)(2,1)} async-done(((bf16[128,2880]{0,1:T(8,128)(2,1)}), bf16[128,2880]{0,1:T(8,128)(2,1)}) %all-reduce.2.cloned.1.call-update) | async-done | bytes 737296 | tf_op jit(solution)/shard_map/psum | solution.py:108
  110.0 1.5 fusion.25
  111.5 7.0 %convolution_convert_fusion = bf16[1536,2880]{0,1:T(8,128)(2,1)} fusion(bf16[196608]{0:T(1024)(128)(2,1)S(1)} %scatter_custom_fusion, bf16[128,2880]{0,1:T(8,128)(2,1)} %all-reduce.2.cloned.1.call-done, f32[2880]{0:T(1024)S(1)} %copy-done.6, f32[128]{0:T(128)S(1)} %add_rsqrt_fusion), kind=kOutput, calls=%fused_computation.24 | convolution fusion | flops 1138360320 | bytes 9989888 | tf_op jit(solution)/shard_map/dot_general | solution.py:142
  118.6 12.5 %copy.89 = bf16[1536,2880]{1,0:T(8,128)(2,1)} copy(bf16[1536,2880]{0,1:T(8,128)(2,1)} %convolution_convert_fusion) | data formatting | bytes 17694720 | tf_op jit(solution)/shard_map/convert_element_type | solution.py:142
  131.0 13.4 %reshape.727 = bf16[8,16,12,2880]{3,2,1,0:T(8,128)(2,1)} reshape(bf16[1536,2880]{1,0:T(8,128)(2,1)} %copy.89) | data formatting | bytes 17694720 | tf_op jit(solution)/shard_map/reshape | solution.py:143
  144.5 9.8 %copy.90 = bf16[8,16,12,2880]{3,1,2,0:T(8,128)(2,1)} copy(bf16[8,16,12,2880]{3,2,1,0:T(8,128)(2,1)} %reshape.727) | data formatting | bytes 17694720 | tf_op jit(solution)/shard_map/reshape | solution.py:143
  154.3 5.5 all-to-all-start
  159.8 55.8 %reshape.728 = bf16[16,180,2,2880]{3,2,0,1:T(2,128)(2,1)} reshape(bf16[16,180,5760]{2,0,1:T(8,128)(2,1)} %param.20) | data formatting | bytes 66355200 | tf_op jit(solution)/shard_map/reshape | solution.py:54
  215.6 140.7 %all-to-all-done = bf16[8,16,12,2880]{3,1,2,0:T(8,128)(2,1)} async-done(((bf16[8,16,12,2880]{3,1,2,0:T(8,128)(2,1)}), bf16[8,16,12,2880]{3,1,2,0:T(8,128)(2,1)}, u32[]{:S(2)}, u32[]{:S(2)}) %all-to-all-start) | async-done | bytes 8847392 | tf_op jit(solution)/shard_map/all_to_all | solution.py:146
  356.3 45.2 %fusion.17 = f32[8,16,12,2,180]{4,2,3,0,1:T(8,128)} fusion(bf16[16,180,2,2880,1]{3,2,0,1,4:T(2,128)(2,1)} %bitcast.102, bf16[8,16,12,2880,1]{3,1,2,0,4:T(8,128)(2,1)} %bitcast.12), kind=kOutput, calls=%fused_computation.28 | convolution fusion | flops 3185049600 | bytes 44236800 | tf_op jit(solution)/shard_map/sgcd,ghzd->sgczh/dot_general | solution.py:144
  401.4 2.8 fusion.24
  405.0 9.5 %collective-permute-done = bf16[8,16,12,180]{3,1,2,0:T(8,128)(2,1)S(1)} collective-permute-done((bf16[8,16,12,180]{3,1,2,0:T(8,128)(2,1)S(1)}, bf16[8,16,12,180]{3,1,2,0:T(8,128)(2,1)S(1)}, u32[]{:S(2)}, u32[]{:S(2)}) %collective-permute-start) | collective-permute-done | bytes 552992 | tf_op jit(solution)/shard_map/ppermute | solution.py:14
  417.2 27.6 %collective-permute-done.1 = bf16[8,16,12,360]{3,1,2,0:T(8,128)(2,1)} collective-permute-done((bf16[8,16,12,360]{3,1,2,0:T(8,128)(2,1)S(1)}, bf16[8,16,12,360]{3,1,2,0:T(8,128)(2,1)}, u32[]{:S(2)}, u32[]{:S(2)}) %collective-permute-start.1) | collective-permute-done | bytes 1105952 | tf_op jit(solution)/shard_map/ppermute | solution.py:14
  444.8 2.8 copy.98
  447.5 11.5 %concatenate.34 = bf16[8,16,12,1440]{3,2,0,1:T(8,128)(2,1)} concatenate(bf16[8,16,12,180]{3,2,0,1:T(8,128)(2,1)S(1)} %fusion.24, bf16[8,16,12,180]{3,2,0,1:T(8,128)(2,1)S(1)} %copy.97, bf16[8,16,12,360]{3,2,0,1:T(8,128)(2,1)} %copy.98, bf16[8,16,12,180]{3,2,0,1:T(8,128)(2,1)S(1)} %fusion.24, bf16[8,16,12,180]{3,2,0,1:T(8,128)(2,1)S(1)} %copy.97, bf16[8,16,12,360]{3,2,0,1:T(8,128)(2,1)} %copy.98), dimensions={3} | concatenate | bytes 8847360 | tf_op jit(solution)/shard_map/jit(_roll_dynamic)/concatenate | solution.py:21
  459.0 9.8 %convert_bitcast_fusion = bf16[8,16,12,720]{3,2,0,1:T(8,128)(2,1)S(1)} fusion(bf16[16,720,720]{2,1,0:T(8,128)(2,1)} %param.21, bf16[8,16,12,1440]{3,2,0,1:T(8,128)(2,1)} %concatenate.34, s32[]{:T(128)S(6)} %select_n.172), kind=kOutput, calls=%fused_computation.26 | convolution fusion | flops 1593630720 | bytes 23052292 | tf_op jit(solution)/shard_map/sgch,ghd->sgcd/dot_general | solution.py:153
  468.9 2.7 copy.101
  471.6 4.5 all-to-all-start.1
  477.9 1.3 fusion.30
  479.4 50.8 %all-to-all-done.1 = bf16[8,16,12,720]{3,1,2,0:T(8,128)(2,1)S(1)} async-done(((bf16[8,16,12,720]{3,1,2,0:T(8,128)(2,1)}), bf16[8,16,12,720]{3,1,2,0:T(8,128)(2,1)S(1)}, u32[]{:S(2)}, u32[]{:S(2)}) %all-to-all-start.1) | async-done | bytes 2211872 | tf_op jit(solution)/shard_map/all_to_all | solution.py:159
  530.2 2.6 copy.102
  532.8 4.0 reshape.729
  536.8 5.2 gather_fusion
  542.0 3.5 reshape.751
  545.5 3.0 multiply_reduce_fusion
  548.5 1.2 copy.104
  (96 shorter events, 15.2 us)
Async XLA Ops:
  6.5 471.4 %copy-start = (bf16[2880,32]{0,1:T(8,128)(2,1)S(1)}, bf16[2880,32]{0,1:T(8,128)(2,1)}, u32[]{:S(2)}) copy-start(bf16[2880,32]{0,1:T(8,128)(2,1)} %param.18) | copy-start | bytes 552964
  6.5 5.1 copy-start.3
  6.5 5.4 copy-start.5
  6.5 21.3 %copy-start.8 = (f32[8]{0:T(128)S(1)}, f32[8]{0:T(128)}, u32[]{:S(2)}) copy-start(f32[8]{0:T(128)} %param.14) | copy-start | bytes 100
  6.5 66.2 %all-gather.2.cloned.1.call-start = ((), (), s32[]{:S(2)}) async-start(), calls=%async_computation.2 | async-start | bytes 3686400 | tf_op jit(solution)/shard_map/all_gather | solution.py:101
  7.3 102.7 %all-reduce.2.cloned.1.call-start = ((), (), s32[]{:S(2)}) async-start(), calls=%async_computation.3 | async-start | bytes 1474560 | tf_op jit(solution)/shard_map/psum | solution.py:108
  27.9 2.5 copy-start.2
  75.5 1.1 copy-start.10
  75.5 1.2 copy-start.9
  75.5 36.0 %copy-start.6 = (f32[2880]{0:T(1024)S(1)}, f32[2880]{0:T(1024)}, u32[]{:S(2)}) copy-start(f32[2880]{0:T(1024)} %param.17) | copy-start | bytes 34564
  111.5 7.1 %copy-start.7 = (f32[128]{0:T(128)}, f32[128]{0:T(128)S(1)}, u32[]{:S(2)}) copy-start(f32[128]{0:T(128)S(1)} %add_rsqrt_fusion) | copy-start | bytes 1540
  154.3 202.0 %all-to-all-start = ((bf16[8,16,12,2880]{3,1,2,0:T(8,128)(2,1)}), bf16[8,16,12,2880]{3,1,2,0:T(8,128)(2,1)}, u32[]{:S(2)}, u32[]{:S(2)}) async-start(bf16[8,16,12,2880]{3,1,2,0:T(8,128)(2,1)} %copy.90), calls=%async_computation | async-start | bytes 18087936 | tf_op jit(solution)/shard_map/all_to_all | solution.py:146
  404.7 9.7 %collective-permute-start = (bf16[8,16,12,180]{3,1,2,0:T(8,128)(2,1)S(1)}, bf16[8,16,12,180]{3,1,2,0:T(8,128)(2,1)S(1)}, u32[]{:S(2)}, u32[]{:S(2)}) collective-permute-start(bf16[8,16,12,180]{3,1,2,0:T(8,128)(2,1)S(1)} %copy.94), channel_id=1, source_target_pairs={{0,6},{2,0},{4,2},{6,4},{1,7},{3,1},{5,3},{7,5},{8,14},{10,8},{12,... | collective-permute-start | bytes 1658888 | tf_op jit(solution)/shard_map/ppermute | solution.py:14
  416.1 28.7 %collective-permute-start.1 = (bf16[8,16,12,360]{3,1,2,0:T(8,128)(2,1)S(1)}, bf16[8,16,12,360]{3,1,2,0:T(8,128)(2,1)}, u32[]{:S(2)}, u32[]{:S(2)}) collective-permute-start(bf16[8,16,12,360]{3,1,2,0:T(8,128)(2,1)S(1)} %copy.96), channel_id=1, source_target_pairs={{0,4},{2,6},{4,0},{6,2},{1,5},{3,7},{5,1},{7,3},{8,12},{10,14},{12... | collective-permute-start | bytes 3317768 | tf_op jit(solution)/shard_map/ppermute | solution.py:14
  471.6 4.5 copy-start.4
  471.6 6.3 %copy-start.1 = (bf16[128,2880]{0,1:T(8,128)(2,1)S(1)}, bf16[128,2880]{0,1:T(8,128)(2,1)}, u32[]{:S(2)}) copy-start(bf16[128,2880]{0,1:T(8,128)(2,1)} %all-reduce.2.cloned.1.call-done) | copy-start | bytes 2211844
  471.6 58.6 %all-to-all-start.1 = ((bf16[8,16,12,720]{3,1,2,0:T(8,128)(2,1)}), bf16[8,16,12,720]{3,1,2,0:T(8,128)(2,1)S(1)}, u32[]{:S(2)}, u32[]{:S(2)}) async-start(bf16[8,16,12,720]{3,1,2,0:T(8,128)(2,1)} %copy.101), calls=%async_computation.1 | async-start | bytes 4718592 | tf_op jit(solution)/shard_map/all_to_all | solution.py:159
Sparse Core Ops, SparseCore 0:
  8.9 63.7 all-gather.1
  76.7 33.2 all-reduce.1
